TPU v7x, 256 devices: a whole 4x4x8 slice. The times are simulated.
256 devices in a mesh: row: 16 (over y, z_lo), col: 16 (over z_hi, x, core).
Axes of the slice: x: 4, y: 4, z: 8 (z_hi: 2, z_lo: 4; z = z_hi * 4 + z_lo), core: 2. Of those that a mesh axis runs over, the one named last changes fastest.
Arguments:
- laplacian: float32 [23040, 23040], P('row', 'col'), may hold values from -1 to 1.12, as said below
- block: float32 [23040, 256], P(('row', 'col')), may hold values from -6 to 6
- bounds: float32 [2], replicated, may hold values from 0.25 to 2.1, as said below
Outputs:
- filtered: float32 [23040, 256], P(('row', 'col'))
- rayleigh: float32 [256, 256], replicated
Inputs may be any that keep to these rules, and one draw needn't show every extreme that they name: laplacian is symmetric; its diagonal entries lie in 0.88 to 1.12 and its other entries have magnitude at most 1.14 / sqrt(23040). bounds[0] lies in 0.25 to 0.40 and bounds[1] in 1.95 to 2.10.
All inputs are finite; a program needn't handle non-finite values.
Results may differ from a plain program's by a relative error of at most 0.00025.
Values sent between devices are 32-bit elements; how exact they have to be, the bound alone decides.
A program may use at most 64 MiB of HBM per device.

v0:
```python
import jax
import jax.numpy as jnp
from jax import lax
from jax.sharding import PartitionSpec as P


def relayout(panel_rows, row_index, col_index, tile_rows, tile_cols):
    offset = col_index * tile_cols - row_index * tile_rows
    zeros_pad = jnp.zeros((tile_cols, panel_rows.shape[1]), jnp.float32)
    padded = jnp.concatenate([zeros_pad, panel_rows, zeros_pad], axis=0)
    start_row = jnp.clip(offset + tile_cols, 0, tile_rows + tile_cols)
    sliced = lax.dynamic_slice_in_dim(padded, start_row, tile_cols, 0)
    target = offset + lax.broadcasted_iota(jnp.int32, (tile_cols, 1), 0)
    inside = (target >= 0) & (target < tile_rows)
    return jnp.where(inside, sliced, 0.0)


def body(laplacian, block, bounds):
    row_index = lax.axis_index("row")
    col_index = lax.axis_index("col")
    tile_rows, tile_cols = laplacian.shape
    lower_bound = bounds[0]
    upper_bound = bounds[1]
    center = (upper_bound + lower_bound) * 0.5
    half_width = (upper_bound - lower_bound) * 0.5
    factor_two = 2.0 / half_width
    global_rows = row_index * tile_rows + lax.broadcasted_iota(jnp.int32, (tile_rows, tile_cols), 0)
    global_cols = col_index * tile_cols + lax.broadcasted_iota(jnp.int32, (tile_rows, tile_cols), 1)
    shifted = laplacian - center * (global_rows == global_cols).astype(jnp.float32)

    def through_columns(panel_rows):
        return lax.dot_general(
            shifted,
            panel_rows,
            (((0,), (0,)), ((), ())),
            precision=lax.Precision.HIGHEST,
            preferred_element_type=jnp.float32,
        )

    def through_rows(panel_cols):
        return jnp.dot(
            shifted, panel_cols, precision=lax.Precision.HIGHEST, preferred_element_type=jnp.float32
        )

    def gather_rows(values):
        return lax.all_gather(values, "col", axis=0, tiled=True)

    def gather_cols(values):
        return lax.all_gather(values, "row", axis=0, tiled=True)

    def column_sum(values):
        return lax.psum_scatter(values, "row", scatter_dimension=0, tiled=True)

    def row_sum(values):
        return lax.psum_scatter(values, "col", scatter_dimension=0, tiled=True)

    filter_one = column_sum(through_columns(gather_rows(block))) / half_width
    filter_two = factor_two * row_sum(through_rows(gather_cols(filter_one))) - block
    filter_three = factor_two * column_sum(through_columns(gather_rows(filter_two))) - filter_one
    filter_four = factor_two * row_sum(through_rows(gather_cols(filter_three))) - filter_two
    panel_four = gather_rows(filter_four)
    dims_inner = (((0,), (0,)), ((), ()))
    image_piece, moved_piece = (
        lax.psum_scatter(through_columns(panel_four), "row", scatter_dimension=0, tiled=True),
        lax.psum_scatter(
            relayout(panel_four, row_index, col_index, tile_rows, tile_cols),
            "row",
            scatter_dimension=0,
            tiled=True,
        ),
    )
    gram_part = lax.dot_general(
        moved_piece,
        moved_piece,
        dims_inner,
        precision=lax.Precision.HIGHEST,
        preferred_element_type=jnp.float32,
    )
    image_part = lax.dot_general(
        moved_piece,
        image_piece,
        dims_inner,
        precision=lax.Precision.HIGHEST,
        preferred_element_type=jnp.float32,
    )
    gram, projected = lax.psum((gram_part, image_part), ("row", "col"))
    projected = projected + center * gram
    projected = (projected + projected.T) * 0.5
    factor = jnp.linalg.cholesky(gram)
    first_solve = jax.scipy.linalg.solve_triangular(factor, projected, lower=True)
    rayleigh = jax.scipy.linalg.solve_triangular(factor, first_solve.T, lower=True)
    return (filter_four, rayleigh)


def solution(mesh):
    placed = (P("row", "col"), P(("row", "col"), None), P())
    return jax.shard_map(
        body, mesh=mesh, in_specs=placed, out_specs=(P(("row", "col"), None), P()), check_vma=False
    )
```

profile of v0, /device:TPU:2, one launch (start us, length us, event | category | flops | bytes accessed | tf_op | source)
XLA Modules:
  0.0 1090.3 jit_solution(2360731310481953332)
XLA Ops:
  7.2 0.7 all-gather.11.cloned.1.call-update
  8.0 1.3 fusion.44
  10.6 61.9 %all-gather.11.cloned.1.call-done = f32[16,90,256]{2,1,0:T(8,128)} async-done(((f32[1,90,256]{2,1,0:T(8,128)}), f32[16,90,256]{2,1,0:T(8,128)}) %all-gather.11.cloned.1.call-update) | async-done | bytes 1474576 | tf_op jit(solution)/shard_map/all_gather | solution.py:46
  72.5 1.5 reshape.61
  74.0 17.9 %fusion.41 = f32[1440,256]{1,0:T(8,128)S(1)} fusion(f32[1440,256]{1,0:T(8,128)S(1)} %reshape.61, f32[1440,1440]{1,0:T(8,128)} %param.5, f32[]{:T(128)} %bitcast.1, s32[1440]{0:T(1024)S(1)} %get-tuple-element.45, s32[1440]{0:T(1024)S(1)} %get-tuple-element.46), kind=kOutput, calls=%fused_computation.71 | convolution fusion | flops 6376320000 | bytes 11255044 | tf_op jit(solution)/shard_map/dot_general | solution.py:32
  91.8 55.3 %fusion = f32[96,256]{1,0:T(8,128)S(1)} fusion(f32[1440,256]{1,0:T(8,128)S(1)} %fusion.41), kind=kCustom, calls=%all-reduce-scatter | all-reduce-scatter fusion | flops 393217 | bytes 1573888
  147.1 1.3 collective-permute-start
  149.7 0.6 dynamic-slice.19
  151.3 0.7 fusion.30
  151.9 0.3 all-gather.15.cloned.1.call-start
  152.2 80.0 %all-gather.13.cloned.1.call-done = f32[16,90,256]{2,1,0:T(8,128)} async-done(((f32[1,90,256]{2,1,0:T(8,128)}), f32[16,90,256]{2,1,0:T(8,128)}) %all-gather.13.cloned.1.call-update) | async-done | bytes 1474576 | tf_op jit(solution)/shard_map/all_gather | solution.py:49
  232.3 1.5 reshape.63
  233.8 10.1 fusion.40
  243.9 48.1 %fusion.1 = f32[96,256]{1,0:T(8,128)S(1)} fusion(f32[1440,256]{1,0:T(8,128)S(1)} %fusion.40), kind=kCustom, calls=%all-reduce-scatter.1 | all-reduce-scatter fusion | flops 393217 | bytes 1573888
  292.0 1.9 collective-permute-start.1
  294.0 0.6 dynamic-slice.23
  295.2 2.7 collective-permute-done.1
  298.2 0.7 fusion.31
  298.9 66.9 %all-gather.15.cloned.1.call-done = f32[16,90,256]{2,1,0:T(8,128)} async-done(((f32[1,90,256]{2,1,0:T(8,128)}), f32[16,90,256]{2,1,0:T(8,128)}) %all-gather.15.cloned.1.call-update) | async-done | bytes 1474576 | tf_op jit(solution)/shard_map/all_gather | solution.py:46
  365.9 1.5 reshape.65
  367.4 17.9 %fusion.39 = f32[1440,256]{1,0:T(8,128)S(1)} fusion(f32[1440,256]{1,0:T(8,128)S(1)} %reshape.65, f32[1440,1440]{1,0:T(8,128)} %param.5, f32[]{:T(128)} %bitcast.1, s32[1440]{0:T(1024)S(1)} %get-tuple-element.45, s32[1440]{0:T(1024)S(1)} %get-tuple-element.46), kind=kOutput, calls=%fused_computation.69 | convolution fusion | flops 6376320000 | bytes 11255044 | tf_op jit(solution)/shard_map/dot_general | solution.py:32
  385.2 55.2 %fusion.2 = f32[96,256]{1,0:T(8,128)S(1)} fusion(f32[1440,256]{1,0:T(8,128)S(1)} %fusion.39), kind=kCustom, calls=%all-reduce-scatter.2 | all-reduce-scatter fusion | flops 393217 | bytes 1573888
  440.4 1.3 collective-permute-start.2
  441.7 2.2 collective-permute-done.2
  444.2 0.7 fusion.18
  444.9 10.4 all-gather.19.cloned.1.call-start
  455.3 70.4 %all-gather.17.cloned.1.call-done = f32[16,90,256]{2,1,0:T(8,128)} async-done(((f32[1,90,256]{2,1,0:T(8,128)}), f32[16,90,256]{2,1,0:T(8,128)}) %all-gather.17.cloned.1.call-update) | async-done | bytes 1474576 | tf_op jit(solution)/shard_map/all_gather | solution.py:49
  525.7 1.5 reshape.67
  527.1 10.1 fusion.38
  537.2 48.0 %fusion.3 = f32[96,256]{1,0:T(8,128)S(1)} fusion(f32[1440,256]{1,0:T(8,128)S(1)} %fusion.38), kind=kCustom, calls=%all-reduce-scatter.3 | all-reduce-scatter fusion | flops 393217 | bytes 1573888
  585.2 1.9 collective-permute-start.3
  587.2 4.0 collective-permute-done.3
  591.4 0.7 fusion.16
  592.2 66.9 %all-gather.19.cloned.1.call-done = f32[16,90,256]{2,1,0:T(8,128)} async-done(((f32[1,90,256]{2,1,0:T(8,128)}), f32[16,90,256]{2,1,0:T(8,128)}) %all-gather.19.cloned.1.call-update) | async-done | bytes 1474576 | tf_op jit(solution)/shard_map/all_gather | solution.py:46
  659.1 1.5 reshape.69
  660.6 19.0 %fusion.37 = f32[1440,256]{1,0:T(8,128)} fusion(f32[1440,256]{1,0:T(8,128)S(1)} %reshape.69, f32[1440,1440]{1,0:T(8,128)} %param.5, f32[]{:T(128)} %bitcast.1, s32[1440]{0:T(1024)S(1)} %get-tuple-element.45, s32[1440]{0:T(1024)S(1)} %get-tuple-element.46), kind=kOutput, calls=%fused_computation.67 | convolution fusion | flops 6376320000 | bytes 11255044 | tf_op jit(solution)/shard_map/dot_general | solution.py:32
  679.7 0.8 fusion.8
  680.5 74.2 %fusion.42 = (f32[96,256]{1,0:T(8,128)S(1)}, f32[96,256]{1,0:T(8,128)S(1)}) fusion(f32[1440,256]{1,0:T(8,128)} %fusion.37, f32[1440,256]{1,0:T(8,128)S(1)} %fusion.8), kind=kCustom, calls=%all-reduce-scatter.6 | all-reduce-scatter fusion | flops 786433 | bytes 3146752
  754.7 1.3 collective-permute-start.4
  756.0 1.5 collective-permute-start.5
  757.5 0.7 collective-permute-done.4
  758.4 1.1 fusion.21
  759.8 1.1 fusion.14
  761.0 256.2 %all-reduce.17.cloned.1.call-done = (f32[256,256]{0,1:T(8,128)}, f32[256,256]{0,1:T(8,128)}) async-done(((f32[256,256]{0,1:T(8,128)}, f32[256,256]{0,1:T(8,128)}), (f32[256,256]{0,1:T(8,128)}, f32[256,256]{0,1:T(8,128)})) %all-reduce.17.cloned.1.call-update) | async-done | bytes 524304 | tf_op jit(solution)/shard_map/psum | solution.py:86
  1017.2 1.1 copy.16
  1018.3 1.1 bitcast_add_fusion.1
  1019.6 11.7 %cholesky.50 = f32[128,128]{1,0:T(8,128)S(1)} custom-call(f32[128,128]{1,0:T(8,128)S(1)} %cholesky.118), custom_call_target="Cholesky" | custom-call | tf_op jit(solution)/shard_map/jit(cholesky)/cholesky | solution.py:89
  1031.4 9.8 custom-call.14
  1041.4 0.3 convolution_subtract_fusion.2
  1041.7 11.7 %cholesky.105 = f32[128,128]{1,0:T(8,128)S(1)} custom-call(f32[128,128]{1,0:T(8,128)S(1)} %convolution_subtract_fusion.2), custom_call_target="Cholesky" | custom-call | tf_op jit(solution)/shard_map/jit(cholesky)/cholesky | solution.py:89
  1053.4 0.7 compare_reduce_fusion
  1054.1 0.6 compare_reduce_fusion.1
  1056.2 4.1 while.4
  1056.2 0.6 fusion.57
  1056.8 1.4 bitcast_dynamic-update-slice_fusion.2
  1058.2 0.6 fusion.57
  1058.8 1.4 bitcast_dynamic-update-slice_fusion.2
  1060.3 19.9 %custom-call.17 = f32[2,128,128]{1,2,0:T(8,128)S(1)} custom-call(f32[2,128,128]{2,1,0:T(8,128)S(1)} %get-tuple-element.18), custom_call_target="InvertDiagBlocksLowerTriangular" | custom-call | tf_op jit(solution)/shard_map/jit(_solve_triangular)/triangular_solve | solution.py:91
  1080.4 0.3 fusion.12
  1080.9 0.3 fusion.27
  1081.3 0.3 fusion.10
  1081.6 0.4 convolution_subtract_fusion
  1082.0 0.3 fusion.26
  1082.3 0.7 pad_maximum_fusion
  (49 shorter events, 3.0 us)
Async XLA Ops:
  7.2 65.3 %all-gather.11.cloned.1.call-start = ((), (), s32[]{:S(2)}) async-start(), calls=%async_computation | async-start | bytes 1671168 | tf_op jit(solution)/shard_map/all_gather | solution.py:46
  7.9 224.4 %all-gather.13.cloned.1.call-start = ((), (), s32[]{:S(2)}) async-start(), calls=%async_computation.1 | async-start | bytes 1671168 | tf_op jit(solution)/shard_map/all_gather | solution.py:49
  91.8 57.9 %copy-start.2 = (u32[256]{0:T(256)S(1)}, u32[256]{0:T(256)}, u32[]{:S(2)}) copy-start(u32[256]{0:T(256)} %constant.130) | copy-start | bytes 3076
  147.1 3.9 collective-permute-start
  151.9 213.9 %all-gather.15.cloned.1.call-start = ((), (), s32[]{:S(2)}) async-start(), calls=%async_computation.2 | async-start | bytes 1671168 | tf_op jit(solution)/shard_map/all_gather | solution.py:46
  243.8 50.1 %copy-start.1 = (u32[256]{0:T(256)S(1)}, u32[256]{0:T(256)}, u32[]{:S(2)}) copy-start(u32[256]{0:T(256)} %constant.134) | copy-start | bytes 3076
  243.9 54.3 %copy-start = (f32[90,256]{1,0:T(8,128)S(1)}, f32[90,256]{1,0:T(8,128)}, u32[]{:S(2)}) copy-start(f32[90,256]{1,0:T(8,128)} %param.6) | copy-start | bytes 276484
  292.0 5.9 collective-permute-start.1
  298.9 226.8 %all-gather.17.cloned.1.call-start = ((), (), s32[]{:S(2)}) async-start(), calls=%async_computation.3 | async-start | bytes 1671168 | tf_op jit(solution)/shard_map/all_gather | solution.py:49
  440.4 3.5 collective-permute-start.2
  444.9 214.2 %all-gather.19.cloned.1.call-start = ((), (), s32[]{:S(2)}) async-start(), calls=%async_computation.4 | async-start | bytes 1671168 | tf_op jit(solution)/shard_map/all_gather | solution.py:46
  585.2 5.9 collective-permute-start.3
  592.1 425.1 %all-reduce.17.cloned.1.call-start = ((), (), s32[]{:S(2)}) async-start(), calls=%async_computation.5 | async-start | bytes 1048576 | tf_op jit(solution)/shard_map/psum | solution.py:86
  754.7 3.5 collective-permute-start.4
  756.0 3.6 collective-permute-start.5
Sparse Core Ops, SparseCore 0:
  10.7 61.7 all-gather.10
  152.1 80.1 all-gather.12
  299.0 66.7 all-gather.14
  445.0 80.5 all-gather.16
  592.3 66.7 all-gather.18
  761.1 256.0 all-reduce.16
where the time goes:
time: 1100 us; the launch traced here: 1090 us
  waiting for transfers between devices  613 us (56%)
  blocking collectives  281 us (26%)
  matrix products  79.5 us (7%)
  other arithmetic  60 us (5%)
  between operations  20.4 us (2%)
  starting transfers between devices  20.1 us (2%)
  local copies, waits for them, and re-layouts  17.1 us (2%)
    unnamed x5, blocking collectives  281 us
    psum x1, waiting for transfers between devices, body(): gram, projected = lax.psum((gram_part, image_part), ('row', 'col'))  256 us
    all_gather x3, waiting for transfers between devices, gather_rows(): return lax.all_gather(values, 'col', axis=0, tiled=True)  196 us
    all_gather x2, waiting for transfers between devices, gather_cols(): return lax.all_gather(values, 'row', axis=0, tiled=True)  150 us
    dot_general x3, matrix products, through_columns(): lax.dot_general(shifted, panel_rows, (((0,), (0,)), ((), ())), precision=...  54.7 us
    another operation x7, other arithmetic, body(): factor = jnp.linalg.cholesky(gram)  34.6 us
  transfers between devices with their start and end apart: 12, of which 10 were waited for; matrix products, arithmetic and copies ran while one was open for 0% of the time, Pallas kernels for 0%

commit v1 on v0

--- a/solution.py
+++ b/solution.py
@@ -2,6 +2,11 @@
 import jax.numpy as jnp
 from jax import lax
 from jax.sharding import PartitionSpec as P
+
+
+def all_by_exchange(block, axis, dim):
+    stack = jnp.stack([block] * lax.axis_size(axis))
+    return jnp.concatenate(lax.all_to_all(stack, axis, 0, 0), axis=dim)
 
 
 def relayout(panel_rows, row_index, col_index, tile_rows, tile_cols):
@@ -43,7 +48,7 @@
         )
 
     def gather_rows(values):
-        return lax.all_gather(values, "col", axis=0, tiled=True)
+        return all_by_exchange(values, "col", 0)
 
     def gather_cols(values):
         return lax.all_gather(values, "row", axis=0, tiled=True)

time: 1100 us -> 1060 us (0.964)
  waiting for transfers between devices: 613 us -> 493 us
  blocking collectives: 281 us -> 349 us
  starting transfers between devices: 20.1 us -> 39.8 us
    all_gather x3 -> x0, waiting for transfers between devices: 196 us -> none  [gather_rows(): return lax.all_gather(values, 'col', axis=0, tiled=True)]
    all_to_all x0 -> x2, waiting for transfers between devices: none -> 55.8 us  [all_by_exchange(): return jnp.concatenate(lax.all_to_all(stack, axis, 0, 0), axis=dim)]
    all_to_all x0 -> x1, blocking collectives: none -> 53.3 us  [all_by_exchange(): return jnp.concatenate(lax.all_to_all(stack, axis, 0, 0), axis=dim)]
    all_to_all x0 -> x2, starting transfers between devices: none -> 29.6 us  [all_by_exchange(): return jnp.concatenate(lax.all_to_all(stack, axis, 0, 0), axis=dim)]
    all_gather x2, waiting for transfers between devices: 150 us -> 170 us  [gather_cols(): return lax.all_gather(values, 'row', axis=0, tiled=True)]
    unnamed x5, blocking collectives: 281 us -> 296 us
  transfers between devices with their start and end apart: 12 -> 11, of which waited for: 10 -> 9; matrix products, arithmetic and copies ran while one was open for 0% -> 0% of each run, Pallas kernels for 0% -> 0%
where the time goes in v1:
time: 1060 us
  waiting for transfers between devices  493 us (47%)
  blocking collectives  349 us (33%)
  matrix products  79.4 us (7%)
  other arithmetic  58.6 us (6%)
  starting transfers between devices  39.8 us (4%)
  between operations  19.7 us (2%)
  local copies, waits for them, and re-layouts  15.8 us (1%)
    unnamed x5, blocking collectives  296 us
    psum x1, waiting for transfers between devices, body(): gram, projected = lax.psum((gram_part, image_part), ('row', 'col'))  257 us
    all_gather x2, waiting for transfers between devices, gather_cols(): return lax.all_gather(values, 'row', axis=0, tiled=True)  170 us
    all_to_all x2, waiting for transfers between devices, all_by_exchange(): return jnp.concatenate(lax.all_to_all(stack, axis, 0, 0), axis=dim)  55.8 us
    dot_general x3, matrix products, through_columns(): lax.dot_general(shifted, panel_rows, (((0,), (0,)), ((), ())), precision=...  54.7 us
    all_to_all x1, blocking collectives, all_by_exchange(): return jnp.concatenate(lax.all_to_all(stack, axis, 0, 0), axis=dim)  53.3 us
    another operation x7, other arithmetic, body(): factor = jnp.linalg.cholesky(gram)  34.6 us
    all_to_all x2, starting transfers between devices, all_by_exchange(): return jnp.concatenate(lax.all_to_all(stack, axis, 0, 0), axis=dim)  29.6 us
  transfers between devices with their start and end apart: 11, of which 9 were waited for; matrix products, arithmetic and copies ran while one was open for 0% of the time, Pallas kernels for 0%

profile of v1, /device:TPU:2, one launch (start us, length us, event | category | flops | bytes accessed | tf_op | source)
XLA Modules:
  0.0 1055.4 jit_solution(17470741312867040194)
XLA Ops:
  7.2 2.2 stack.6
  9.4 11.6 %all-to-all-start = ((f32[16,90,256]{2,1,0:T(8,128)}), f32[16,90,256]{2,1,0:T(8,128)S(1)}, u32[]{:S(2)}, u32[]{:S(2)}) async-start(f32[16,90,256]{2,1,0:T(8,128)} %stack.6), calls=%async_computation | async-start | bytes 3145728 | tf_op jit(solution)/shard_map/all_to_all | solution.py:9
  21.0 0.6 fusion.43
  22.9 21.2 %all-to-all-done = f32[16,90,256]{2,1,0:T(8,128)S(1)} async-done(((f32[16,90,256]{2,1,0:T(8,128)}), f32[16,90,256]{2,1,0:T(8,128)S(1)}, u32[]{:S(2)}, u32[]{:S(2)}) %all-to-all-start) | async-done | bytes 1474592 | tf_op jit(solution)/shard_map/all_to_all | solution.py:9
  44.3 17.9 %fusion.40 = f32[1440,256]{1,0:T(8,128)S(1)} fusion(f32[1440,256]{1,0:T(8,128)S(1)} %reshape.53, f32[1440,1440]{1,0:T(8,128)} %param.5, f32[]{:T(128)} %bitcast.1, s32[1440]{0:T(1024)S(1)} %get-tuple-element.45, s32[1440]{0:T(1024)S(1)} %get-tuple-element.46), kind=kOutput, calls=%fused_computation.70 | convolution fusion | flops 6376320000 | bytes 11255044 | tf_op jit(solution)/shard_map/dot_general | solution.py:37
  62.1 69.7 %fusion = f32[96,256]{1,0:T(8,128)S(1)} fusion(f32[1440,256]{1,0:T(8,128)S(1)} %fusion.40), kind=kCustom, calls=%all-reduce-scatter | all-reduce-scatter fusion | flops 393217 | bytes 1573888
  131.8 1.3 collective-permute-start
  134.4 0.6 dynamic-slice.19
  135.7 0.3 concatenate.7
  136.0 0.7 fusion.30
  136.9 84.2 %all-gather.5.cloned.1.call-done = f32[16,90,256]{2,1,0:T(8,128)} async-done(((f32[1,90,256]{2,1,0:T(8,128)}), f32[16,90,256]{2,1,0:T(8,128)}) %all-gather.5.cloned.1.call-update) | async-done | bytes 1474576 | tf_op jit(solution)/shard_map/all_gather | solution.py:54
  221.1 1.5 reshape.79
  222.6 10.1 fusion.39
  232.7 48.1 %fusion.1 = f32[96,256]{1,0:T(8,128)S(1)} fusion(f32[1440,256]{1,0:T(8,128)S(1)} %fusion.39), kind=kCustom, calls=%all-reduce-scatter.1 | all-reduce-scatter fusion | flops 393217 | bytes 1573888
  280.8 1.9 collective-permute-start.1
  282.8 0.6 dynamic-slice.23
  284.1 2.7 collective-permute-done.1
  287.2 53.3 %all_to_all.15 = f32[16,90,256]{2,1,0:T(8,128)S(1)} all-to-all(f32[16,90,256]{2,1,0:T(8,128)S(1)} %stack.7), channel_id=1, replica_groups=mesh['row'=16,'col'=16] {'col'}, dimensions={0} | all-to-all | bytes 2949120 | tf_op jit(solution)/shard_map/all_to_all | solution.py:9
  340.7 17.9 %fusion.38 = f32[1440,256]{1,0:T(8,128)S(1)} fusion(f32[1440,256]{1,0:T(8,128)S(1)} %reshape.54, f32[1440,1440]{1,0:T(8,128)} %param.5, f32[]{:T(128)} %bitcast.1, s32[1440]{0:T(1024)S(1)} %get-tuple-element.45, s32[1440]{0:T(1024)S(1)} %get-tuple-element.46), kind=kOutput, calls=%fused_computation.68 | convolution fusion | flops 6376320000 | bytes 11255044 | tf_op jit(solution)/shard_map/dot_general | solution.py:37
  358.6 54.4 %fusion.2 = f32[96,256]{1,0:T(8,128)S(1)} fusion(f32[1440,256]{1,0:T(8,128)S(1)} %fusion.38), kind=kCustom, calls=%all-reduce-scatter.2 | all-reduce-scatter fusion | flops 393217 | bytes 1573888
  413.0 1.6 collective-permute-start.2
  414.5 1.9 collective-permute-done.2
  416.7 0.7 fusion.18
  417.4 86.0 %all-gather.7.cloned.1.call-done = f32[16,90,256]{2,1,0:T(8,128)} async-done(((f32[1,90,256]{2,1,0:T(8,128)}), f32[16,90,256]{2,1,0:T(8,128)}) %all-gather.7.cloned.1.call-update) | async-done | bytes 1474576 | tf_op jit(solution)/shard_map/all_gather | solution.py:54
  503.5 1.5 reshape.81
  504.9 10.1 fusion.37
  515.0 48.0 %fusion.3 = f32[96,256]{1,0:T(8,128)S(1)} fusion(f32[1440,256]{1,0:T(8,128)S(1)} %fusion.37), kind=kCustom, calls=%all-reduce-scatter.3 | all-reduce-scatter fusion | flops 393217 | bytes 1573888
  563.0 1.9 collective-permute-start.3
  565.0 4.0 collective-permute-done.3
  569.3 1.3 stack.8
  570.6 18.0 %all-to-all-start.2 = ((f32[16,90,256]{2,1,0:T(8,128)}), f32[16,90,256]{2,1,0:T(8,128)S(1)}, u32[]{:S(2)}, u32[]{:S(2)}) async-start(f32[16,90,256]{2,1,0:T(8,128)} %stack.8), calls=%async_computation.2 | async-start | bytes 3145728 | tf_op jit(solution)/shard_map/all_to_all | solution.py:9
  588.5 0.5 all-reduce.17.cloned.1.call-start
  589.1 34.6 %all-to-all-done.2 = f32[16,90,256]{2,1,0:T(8,128)S(1)} async-done(((f32[16,90,256]{2,1,0:T(8,128)}), f32[16,90,256]{2,1,0:T(8,128)S(1)}, u32[]{:S(2)}, u32[]{:S(2)}) %all-to-all-start.2) | async-done | bytes 1474592 | tf_op jit(solution)/shard_map/all_to_all | solution.py:9
  623.9 19.0 %fusion.36 = f32[1440,256]{1,0:T(8,128)} fusion(f32[1440,256]{1,0:T(8,128)S(1)} %reshape.55, f32[1440,1440]{1,0:T(8,128)} %param.5, f32[]{:T(128)} %bitcast.1, s32[1440]{0:T(1024)S(1)} %get-tuple-element.45, s32[1440]{0:T(1024)S(1)} %get-tuple-element.46), kind=kOutput, calls=%fused_computation.66 | convolution fusion | flops 6376320000 | bytes 11255044 | tf_op jit(solution)/shard_map/dot_general | solution.py:37
  643.0 0.8 fusion.8
  643.8 75.7 %fusion.41 = (f32[96,256]{1,0:T(8,128)S(1)}, f32[96,256]{1,0:T(8,128)S(1)}) fusion(f32[1440,256]{1,0:T(8,128)} %fusion.36, f32[1440,256]{1,0:T(8,128)S(1)} %fusion.8), kind=kCustom, calls=%all-reduce-scatter.6 | all-reduce-scatter fusion | flops 786433 | bytes 3146752
  719.5 1.3 collective-permute-start.4
  720.8 1.5 collective-permute-start.5
  722.3 0.7 collective-permute-done.4
  723.3 1.1 fusion.21
  724.4 0.3 concatenate.12
  724.6 1.1 fusion.14
  725.8 257.5 %all-reduce.17.cloned.1.call-done = (f32[256,256]{0,1:T(8,128)}, f32[256,256]{0,1:T(8,128)}) async-done(((f32[256,256]{0,1:T(8,128)}, f32[256,256]{0,1:T(8,128)}), (f32[256,256]{0,1:T(8,128)}, f32[256,256]{0,1:T(8,128)})) %all-reduce.17.cloned.1.call-update) | async-done | bytes 524304 | tf_op jit(solution)/shard_map/psum | solution.py:91
  983.3 1.1 copy.16
  984.3 1.1 bitcast_add_fusion.1
  985.6 11.7 %cholesky.50 = f32[128,128]{1,0:T(8,128)S(1)} custom-call(f32[128,128]{1,0:T(8,128)S(1)} %cholesky.118), custom_call_target="Cholesky" | custom-call | tf_op jit(solution)/shard_map/jit(cholesky)/cholesky | solution.py:94
  997.4 9.8 custom-call.14
  1007.4 0.3 convolution_subtract_fusion.2
  1007.7 11.7 %cholesky.105 = f32[128,128]{1,0:T(8,128)S(1)} custom-call(f32[128,128]{1,0:T(8,128)S(1)} %convolution_subtract_fusion.2), custom_call_target="Cholesky" | custom-call | tf_op jit(solution)/shard_map/jit(cholesky)/cholesky | solution.py:94
  1019.4 0.6 compare_reduce_fusion
  1020.1 0.6 compare_reduce_fusion.1
  1022.0 3.8 while.4
  1022.0 0.6 fusion.56
  1022.6 1.3 bitcast_dynamic-update-slice_fusion.2
  1024.0 0.6 fusion.56
  1024.5 1.3 bitcast_dynamic-update-slice_fusion.2
  1025.8 19.9 %custom-call.17 = f32[2,128,128]{1,2,0:T(8,128)S(1)} custom-call(f32[2,128,128]{2,1,0:T(8,128)S(1)} %get-tuple-element.18), custom_call_target="InvertDiagBlocksLowerTriangular" | custom-call | tf_op jit(solution)/shard_map/jit(_solve_triangular)/triangular_solve | solution.py:96
  1045.9 0.3 fusion.12
  1046.2 0.3 convolution_subtract_fusion.1
  1046.5 0.3 fusion.27
  1046.9 0.3 fusion.10
  1047.2 0.4 convolution_subtract_fusion
  1047.6 0.3 fusion.26
  1047.9 0.7 pad_maximum_fusion
  (52 shorter events, 3.0 us)
Async XLA Ops:
  9.4 11.7 %copy-start.2 = (f32[2]{0:T(128)S(1)}, f32[2]{0:T(128)}, u32[]{:S(2)}) copy-start(f32[2]{0:T(128)} %param.7) | copy-start | bytes 28
  9.4 34.7 %all-to-all-start = ((f32[16,90,256]{2,1,0:T(8,128)}), f32[16,90,256]{2,1,0:T(8,128)S(1)}, u32[]{:S(2)}, u32[]{:S(2)}) async-start(f32[16,90,256]{2,1,0:T(8,128)} %stack.6), calls=%async_computation | async-start | bytes 3145728 | tf_op jit(solution)/shard_map/all_to_all | solution.py:9
  21.0 200.1 %all-gather.5.cloned.1.call-start = ((), (), s32[]{:S(2)}) async-start(), calls=%async_computation.3 | async-start | bytes 1671168 | tf_op jit(solution)/shard_map/all_gather | solution.py:54
  62.1 72.3 %copy-start.4 = (u32[256]{0:T(256)S(1)}, u32[256]{0:T(256)}, u32[]{:S(2)}) copy-start(u32[256]{0:T(256)} %constant.130) | copy-start | bytes 3076
  131.8 3.9 collective-permute-start
  136.6 366.8 %all-gather.7.cloned.1.call-start = ((), (), s32[]{:S(2)}) async-start(), calls=%async_computation.4 | async-start | bytes 1671168 | tf_op jit(solution)/shard_map/all_gather | solution.py:54
  232.7 50.1 %copy-start.3 = (u32[256]{0:T(256)S(1)}, u32[256]{0:T(256)}, u32[]{:S(2)}) copy-start(u32[256]{0:T(256)} %constant.134) | copy-start | bytes 3076
  232.7 54.3 %copy-start = (f32[90,256]{1,0:T(8,128)S(1)}, f32[90,256]{1,0:T(8,128)}, u32[]{:S(2)}) copy-start(f32[90,256]{1,0:T(8,128)} %param.6) | copy-start | bytes 276484
  280.8 5.9 collective-permute-start.1
  413.0 3.5 collective-permute-start.2
  563.0 5.9 collective-permute-start.3
  569.3 1.3 copy-start.1
  570.6 53.1 %all-to-all-start.2 = ((f32[16,90,256]{2,1,0:T(8,128)}), f32[16,90,256]{2,1,0:T(8,128)S(1)}, u32[]{:S(2)}, u32[]{:S(2)}) async-start(f32[16,90,256]{2,1,0:T(8,128)} %stack.8), calls=%async_computation.2 | async-start | bytes 3145728 | tf_op jit(solution)/shard_map/all_to_all | solution.py:9
  588.5 394.7 %all-reduce.17.cloned.1.call-start = ((), (), s32[]{:S(2)}) async-start(), calls=%async_computation.5 | async-start | bytes 1048576 | tf_op jit(solution)/shard_map/psum | solution.py:91
  719.5 3.5 collective-permute-start.4
  720.8 3.5 collective-permute-start.5
Sparse Core Ops, SparseCore 0:
  136.8 84.2 all-gather.4
  417.5 85.8 all-gather.6
  725.9 257.3 all-reduce.16
